TPU v7x, 256 devices: a whole 4x4x8 slice. The times are simulated.
256 devices in a mesh: row: 32 (over z, x), col: 8 (over y, core).
Axes of the slice: x: 4, y: 4, z: 8, core: 2. Of those that a mesh axis runs over, the one named last changes fastest.
Arguments:
- schur: float32 [2, 32768, 4096], P(None, 'row', 'col'), may hold values from -6 to 6
- lower: bfloat16 [2, 32768, 2048], P(None, 'row', 'col'), may hold values from -6 to 6
- upper: bfloat16 [2, 2048, 4096], P(None, 'row', 'col'), may hold values from -0.1875 to 0.1875
- tile_mask: int32 [2, 256, 16], P(None, 'row', 'col'), may hold values from 0 to 1, as said below
- row_map: int32 [2, 32768], P(None, 'row'), may hold values from 0 to 32767, as said below
- front: float32 [32768, 4096], P('row', 'col'), may hold values from -6 to 6
Outputs:
- front_out: float32 [32768, 4096], P('row', 'col')
Inputs may be any that keep to these rules, and one draw needn't show every extreme that they name: `tile_mask`: in every row of tiles of each child, each aligned pair of tile columns (2 j, 2 j + 1) holds exactly one 1. `row_map`: for each child a permutation of the 32768 rows. Of the 1024 rows of any aligned block, at least 16 and at most 48 map into any one aligned block of 1024 parent rows; some pair of blocks reaches 48.
All inputs are finite; a program needn't handle non-finite values.
Results may differ from a plain program's by a relative error of at most 0.0003.
Values may be sent and summed in bfloat16 or wider, within the bound.
A program may use at most 128 MiB of HBM per device.

v0:
```python
import jax
import jax.numpy as jnp
from jax import lax
from jax.sharding import Mesh
from jax.sharding import PartitionSpec as P

TILE = 128
ROW = ("row_0", "row_1")


def gathered_by_axis(array, axes, dim):
    result = array
    for number in range(len(axes) - 1, -1, -1):
        result = lax.all_gather(result, axes[number], axis=dim, tiled=True)
    return result


def build_send(contrib, maps, count):
    children, rows, width = contrib.shape
    cap = 3 * rows // (2 * count)
    target = maps // rows
    place = maps % rows
    onehot = (target[:, :, None] == jnp.arange(count, dtype=jnp.int32)[None, None, :]).astype(
        jnp.int32
    )
    ranks = jnp.cumsum(onehot, axis=1) - 1
    slot = jnp.sum(ranks * onehot, axis=2)
    flat = target * cap + slot
    child_ids = jnp.arange(children, dtype=jnp.int32)[:, None]
    values = jnp.zeros((children, count * cap, width), jnp.float32).at[child_ids, flat].set(contrib)
    places = (
        jnp.full((children, count * cap), float(rows), jnp.float32)
        .at[child_ids, flat]
        .set(place.astype(jnp.float32))
    )
    return (values.reshape(children, count, cap, width), places.reshape(children, count, cap))


def assemble(result, values, places):
    width = values.shape[-1]
    index = places.reshape(-1).astype(jnp.int32)
    return result.at[index].add(values.reshape(-1, width), mode="drop")


def shards(schur, lower, upper, tile_mask, row_map, front):
    children, rows, local_depth = lower.shape
    width = schur.shape[2]
    row_tiles = rows // TILE
    local_tiles = local_depth // TILE
    upper_full = gathered_by_axis(upper, ROW, 1)
    local_pairs = local_tiles // 2
    lower_six = lower.reshape(children, row_tiles, TILE, local_pairs, 2, TILE)
    weight_six = tile_mask.reshape(children, row_tiles, 1, local_pairs, 2, 1).astype(jnp.bfloat16)
    packed = jnp.sum(lower_six * weight_six, axis=4).reshape(children, rows, local_pairs * TILE)
    flags = tile_mask.reshape(children, row_tiles, local_pairs, 2)[..., 1].astype(jnp.bfloat16)
    packed_full, flags_full = (
        lax.all_gather(packed, "col", axis=2, tiled=True),
        lax.all_gather(flags, "col", axis=2, tiled=True),
    )
    total_pairs = flags_full.shape[2]
    upper_pairs = upper_full.reshape(children, total_pairs, 2, TILE, width)
    packed_five = packed_full.reshape(children, row_tiles, TILE, total_pairs, TILE)
    update = jnp.zeros((children, rows, width), jnp.float32)
    for parity in range(2):
        select = (flags_full == float(parity)).astype(jnp.bfloat16)
        chosen = (packed_five * select[:, :, None, :, None]).reshape(
            children, rows, total_pairs * TILE
        )
        panel = upper_pairs[:, :, parity].reshape(children, total_pairs * TILE, width)
        update = update + jnp.einsum(
            "cmk,ckw->cmw", chosen, panel, preferred_element_type=jnp.float32
        )
    contrib = schur - update
    count = lax.axis_size(ROW)
    result = front
    values, places = build_send(contrib, row_map, count)
    got_values, got_places = (
        lax.all_to_all(values, ROW, split_axis=1, concat_axis=1, tiled=True),
        lax.all_to_all(places, ROW, split_axis=1, concat_axis=1, tiled=True),
    )
    result = assemble(result, got_values, got_places)
    return result


def solution(mesh):
    split = Mesh(mesh.devices.reshape(8, 4, mesh.shape["col"]), ("row_0", "row_1", "col"))
    in_specs = (
        P(None, ROW, "col"),
        P(None, ROW, "col"),
        P(None, ROW, "col"),
        P(None, ROW, "col"),
        P(None, ROW),
        P(ROW, "col"),
    )
    out_specs = P(ROW, "col")
    return jax.shard_map(
        shards, mesh=split, in_specs=in_specs, out_specs=out_specs, check_vma=False
    )
```

profile of v0, /device:TPU:103, one launch (start us, length us, event | category | flops | bytes accessed | tf_op | source)
XLA Modules:
  0.0 343.6 jit_solution(4166249342058747314)
XLA Ops:
  6.5 0.0 all-gather.6.cloned.1.call-start
  6.6 3.2 copy.65
  9.8 0.0 copy-done.4
  9.8 10.8 %all_gather.14 = bf16[2,256,512]{2,1,0:T(8,128)(2,1)} all-gather(bf16[2,64,512]{2,1,0:T(8,128)(2,1)S(1)} %copy-done.4), channel_id=1, replica_groups=mesh['row_0'=8,'row_1'=4,'col'=8] {'row_1'}, dimensions={1}, use_global_device_ids=true | all-gather | bytes 655360 | tf_op jit(solution)/shard_map/all_gather | solution.py:14
  20.5 0.0 all-gather.6.cloned.1.call-update
  20.5 0.0 all-gather.4.cloned.1.call-start
  20.6 0.0 copy-done.3
  20.6 0.3 reshape.99
  20.9 0.0 copy-done.6
  20.9 0.1 copy.43
  21.0 3.7 %multiply_reduce_fusion = bf16[2,8,128,128]{3,2,1,0:T(8,128)(2,1)} fusion(bf16[2,8,128,1,2,128]{5,4,2,1,0,3:T(2,128)(2,1)S(1)} %reshape.99, bf16[2,8,2]{2,1,0:T(8,128)(2,1)S(1)} %copy.43), kind=kLoop, calls=%fused_computation.10 | loop fusion | flops 786432 | bytes 1572928 | tf_op jit(solution)/shard_map/reduce_sum | solution.py:54
  24.8 0.0 all-gather.4.cloned.1.call-update
  24.8 0.0 copy-done.5
  24.9 18.0 %reduce-window.6 = s32[2,32,8,128]{3,2,1,0:T(8,128)S(1)} reduce-window(s32[2,32,8,128]{3,2,1,0:T(8,128)S(1)} %fusion.9, s32[]{:T(128)} %constant.45.clone.1), window={size=1x1x1x128 pad=0_0x0_0x0_0x127_0}, to_apply=%region_0.0 | reduce-window | flops 8323072 | bytes 524292 | tf_op jit(solution)/shard_map/reduce-window
  42.9 0.1 slice.21
  43.0 0.2 copy.39
  43.3 0.1 copy.40
  43.3 0.1 add_add_fusion
  43.5 0.1 fusion.8
  43.6 0.0 copy-done.7
  43.6 0.1 multiply_reduce_fusion.1
  43.7 0.0 copy-done.8
  43.7 0.1 and_reduce_fusion
  43.9 8.1 %scatter_custom_fusion.1 = f32[3072]{0:T(1024)S(1)} fusion(s32[2048]{0:T(1024)S(1)} %bitcast.58, f32[2048]{0:T(1024)S(1)} %bitcast.60, f32[]{:T(128)} %constant.43.clone.1), kind=kCustom, calls=%fused_computation.37 | custom fusion | bytes 12292
  51.9 0.1 reshape.98
  52.0 0.6 copy.41
  52.6 9.4 %all-to-all-start = ((f32[2,32,48]{2,0,1:T(2,128)}), f32[2,32,48]{2,0,1:T(2,128)S(1)}, u32[]{:S(2)}, u32[]{:S(2)}) async-start(f32[2,32,48]{2,0,1:T(2,128)} %copy.41), calls=%async_computation | async-start | bytes 65536 | tf_op jit(solution)/shard_map/all_to_all | solution.py:79
  62.1 15.6 %all-gather = bf16[2,8,8,1]{1,0,3,2:T(2,128)(2,1)S(1)} all-gather(bf16[2,8,1,1]{1,0,3,2:T(2,128)(2,1)S(1)} %copy.44), channel_id=2, replica_groups=mesh['row_0'=8,'row_1'=4,'col'=8] {'col'}, dimensions={2}, use_global_device_ids=true | all-gather | bytes 288 | tf_op jit(solution)/shard_map/all_gather | solution.py:58
  77.7 0.1 copy.45
  77.8 2.6 mul.55
  80.3 7.3 %mul.56 = bf16[2,1024,1024]{2,1,0:T(8,128)(2,1)} reshape(bf16[2,8,128,8,128]{4,3,2,1,0:T(8,128)(2,1)} %mul.55) | data formatting | bytes 8388608 | tf_op jit(solution)/shard_map/mul | solution.py:66
  87.7 2.5 mul.52
  90.2 7.3 %mul.53 = bf16[2,1024,1024]{2,1,0:T(8,128)(2,1)} reshape(bf16[2,8,128,8,128]{4,3,2,1,0:T(8,128)(2,1)} %mul.52) | data formatting | bytes 8388608 | tf_op jit(solution)/shard_map/mul | solution.py:66
  97.5 4.0 %fusion.17 = (bf16[2,8,1,128,512]{4,3,2,1,0:T(8,128)(2,1)S(1)}, bf16[2,8,1,128,512]{4,3,2,1,0:T(8,128)(2,1)}) fusion(bf16[2,8,2,128,512]{4,3,2,1,0:T(8,128)(2,1)} %bitcast.50), kind=kLoop, calls=%fused_computation.43 | loop fusion | bytes 8388608 | tf_op jit(solution)/shard_map/slice | solution.py:69
  101.5 18.7 %all-gather.4.cloned.1.call-done = bf16[2,1024,1024]{2,1,0:T(8,128)(2,1)} async-done(((bf16[2,1024,128]{2,1,0:T(8,128)(2,1)}), bf16[2,1024,1024]{2,1,0:T(8,128)(2,1)}) %all-gather.4.cloned.1.call-update) | async-done | bytes 4194320 | tf_op jit(solution)/shard_map/all_gather | solution.py:57
  120.2 6.5 %fusion = f32[2,1024,512]{2,1,0:T(8,128)S(1)} fusion(bf16[2,1024,512]{2,1,0:T(8,128)(2,1)} %bitcast.53, bf16[2,1024,1024]{2,1,0:T(8,128)(2,1)} %all-gather.4.cloned.1.call-done, bf16[2,1024,1024]{2,1,0:T(8,128)(2,1)} %mul.56), kind=kOutput, calls=%fused_computation.4 | convolution fusion | flops 2149580800 | bytes 14680064 | tf_op jit(solution)/shard_map/cmk,ckw->cmw/dot_general | solution.py:70
  126.8 0.0 copy-done
  126.8 0.0 copy-done.1
  126.8 1.2 copy-done.2
  128.0 4.3 %add_subtract_fusion = f32[2,1024,512]{2,1,0:T(8,128)} fusion(f32[2,1024,512]{2,1,0:T(8,128)S(1)} %copy-done.1, f32[2,1024,512]{2,1,0:T(8,128)S(1)} %fusion, bf16[2,1024,512]{2,1,0:T(8,128)(2,1)S(1)} %bitcast.49, bf16[2,1024,1024]{2,1,0:T(8,128)(2,1)S(1)} %copy-done.2, bf16[2,1024,1024]{2,1,0:T(8,128)(2,1)S(1)} %copy-done), kind=kOutput, calls=%fused_computation.3 | convolution fusion | flops 2151677952 | bytes 23068672 | tf_op jit(solution)/shard_map/cmk,ckw->cmw/dot_general | solution.py:70
  132.2 12.7 %scatter_custom_fusion.2 = f32[3072,512]{1,0:T(8,128)} fusion(s32[2048]{0:T(1024)S(1)} %bitcast.59, f32[2048,512]{1,0:T(8,128)} %bitcast.51, f32[]{:T(128)} %constant.52.clone.1), kind=kCustom, calls=%fused_computation.8 | custom fusion | bytes 6291968
  144.9 6.7 %copy.49 = f32[2,32,48,512]{3,2,0,1:T(8,128)} copy(f32[2,32,48,512]{3,2,1,0:T(8,128)} %bitcast.47) | data formatting | bytes 12582912 | tf_op jit(solution)/shard_map/reshape | solution.py:36
  151.6 0.0 all-to-all-done
  151.6 9.4 %all-to-all-start.1 = ((f32[2,32,48,512]{3,2,0,1:T(8,128)}), f32[2,32,48,512]{3,2,0,1:T(8,128)}, u32[]{:S(2)}, u32[]{:S(2)}) async-start(f32[2,32,48,512]{3,2,0,1:T(8,128)} %copy.49), calls=%async_computation.1 | async-start | bytes 12582912 | tf_op jit(solution)/shard_map/all_to_all | solution.py:78
  161.0 0.1 convert_element_type.48
  161.1 146.8 %all-to-all-done.1 = f32[2,32,48,512]{3,2,0,1:T(8,128)} async-done(((f32[2,32,48,512]{3,2,0,1:T(8,128)}), f32[2,32,48,512]{3,2,0,1:T(8,128)}, u32[]{:S(2)}, u32[]{:S(2)}) %all-to-all-start.1) | async-done | bytes 6291488 | tf_op jit(solution)/shard_map/all_to_all | solution.py:78
  308.0 6.8 %copy.50 = f32[2,32,48,512]{3,2,1,0:T(8,128)} copy(f32[2,32,48,512]{3,2,0,1:T(8,128)} %all-to-all-done.1) | data formatting | bytes 12582912 | tf_op jit(solution)/shard_map/all_to_all | solution.py:78
  314.7 22.1 %scatter_fusion = f32[1024,512]{1,0:T(8,128)} fusion(f32[1024,512]{1,0:T(8,128)} %copy.65, s32[3072]{0:T(1024)S(1)} %bitcast.55, f32[3072,512]{1,0:T(8,128)} %bitcast.48), kind=kCustom, calls=%fused_computation | custom fusion | flops 1572864 | bytes 18886656 | tf_op jit(solution)/shard_map/scatter-add | solution.py:42
  (28 shorter events, 0.2 us)
Async XLA Ops:
  6.5 3.2 copy-start.4
  6.5 14.1 %copy-start.3 = (bf16[2,1024,256]{2,1,0:T(8,128)(2,1)S(1)}, bf16[2,1024,256]{2,1,0:T(8,128)(2,1)}, u32[]{:S(2)}) copy-start(bf16[2,1024,256]{2,1,0:T(8,128)(2,1)} %param.7) | copy-start | bytes 3145732
  6.5 14.4 %copy-start.6 = (s32[2,8,2]{1,2,0:T(2,128)S(1)}, s32[2,8,2]{1,2,0:T(2,128)}, u32[]{:S(2)}) copy-start(s32[2,8,2]{1,2,0:T(2,128)} %param.9) | copy-start | bytes 388
  6.5 18.3 %copy-start.5 = (s32[2,1024]{1,0:T(2,128)S(1)}, s32[2,1024]{1,0:T(2,128)}, u32[]{:S(2)}) copy-start(s32[2,1024]{1,0:T(2,128)} %param.10) | copy-start | bytes 24580
  6.5 91.0 %all-gather.6.cloned.1.call-start = ((), (), s32[]{:S(2)}) async-start(), calls=%async_computation.3 | async-start | bytes 4718592 | tf_op jit(solution)/shard_map/all_gather | solution.py:14
  9.8 33.9 %copy-start.7 = (s32[2]{0:T(128)S(1)}, s32[2]{0:T(128)}, u32[]{:S(2)}) copy-start(s32[2]{0:T(128)} %constant.56) | copy-start | bytes 28
  9.8 34.0 %copy-start.8 = (s32[2]{0:T(128)S(1)}, s32[2]{0:T(128)}, u32[]{:S(2)}) copy-start(s32[2]{0:T(128)} %constant.59) | copy-start | bytes 28
  20.5 99.7 %all-gather.4.cloned.1.call-start = ((), (), s32[]{:S(2)}) async-start(), calls=%async_computation.2 | async-start | bytes 4718592 | tf_op jit(solution)/shard_map/all_gather | solution.py:57
  52.6 99.0 %all-to-all-start = ((f32[2,32,48]{2,0,1:T(2,128)}), f32[2,32,48]{2,0,1:T(2,128)S(1)}, u32[]{:S(2)}, u32[]{:S(2)}) async-start(f32[2,32,48]{2,0,1:T(2,128)} %copy.41), calls=%async_computation | async-start | bytes 65536 | tf_op jit(solution)/shard_map/all_to_all | solution.py:79
  120.2 6.5 %copy-start = (bf16[2,1024,1024]{2,1,0:T(8,128)(2,1)S(1)}, bf16[2,1024,1024]{2,1,0:T(8,128)(2,1)}, u32[]{:S(2)}) copy-start(bf16[2,1024,1024]{2,1,0:T(8,128)(2,1)} %mul.53) | copy-start | bytes 12582916
  120.2 6.5 %copy-start.1 = (f32[2,1024,512]{2,1,0:T(8,128)S(1)}, f32[2,1024,512]{2,1,0:T(8,128)}, u32[]{:S(2)}) copy-start(f32[2,1024,512]{2,1,0:T(8,128)} %param.6) | copy-start | bytes 12582916
  120.2 7.7 %copy-start.2 = (bf16[2,1024,1024]{2,1,0:T(8,128)(2,1)S(1)}, bf16[2,1024,1024]{2,1,0:T(8,128)(2,1)}, u32[]{:S(2)}) copy-start(bf16[2,1024,1024]{2,1,0:T(8,128)(2,1)} %all-gather.4.cloned.1.call-done) | copy-start | bytes 12582916
  151.6 156.3 %all-to-all-start.1 = ((f32[2,32,48,512]{3,2,0,1:T(8,128)}), f32[2,32,48,512]{3,2,0,1:T(8,128)}, u32[]{:S(2)}, u32[]{:S(2)}) async-start(f32[2,32,48,512]{3,2,0,1:T(8,128)} %copy.49), calls=%async_computation.1 | async-start | bytes 12582912 | tf_op jit(solution)/shard_map/all_to_all | solution.py:78
Sparse Core Ops, SparseCore 0:
  20.7 59.8 all-gather.5
  82.4 37.8 all-gather.3
where the time goes:
time: 344 us
  waiting for transfers between devices  166 us (48%)
  local copies, waits for them, and re-layouts  64 us (19%)
  other arithmetic  44.3 us (13%)
  blocking collectives  26.3 us (8%)
  starting transfers between devices  18.9 us (5%)
  between operations  13.7 us (4%)
  matrix products  10.8 us (3%)
    all_to_all x1, waiting for transfers between devices, shards(): lax.all_to_all(values, ROW, split_axis=1, concat_axis=1, tiled=True)  147 us
    unnamed x24, local copies, waits for them, and re-layouts  25.1 us
    scatter-add x1, other arithmetic, assemble(): return result.at[index].add(values.reshape(-1, width), mode='drop')  22.1 us
    mul x4, local copies, waits for them, and re-layouts, shards(): packed_five * select[:, :, None, :, None]  19.8 us
    all_gather x1, waiting for transfers between devices, shards(): lax.all_gather(packed, 'col', axis=2, tiled=True)  18.7 us
    another operation x2, other arithmetic  18.1 us
    all_gather x1, blocking collectives, shards(): lax.all_gather(flags, 'col', axis=2, tiled=True)  15.6 us
    dot_general x2, matrix products, shards(): jnp.einsum('cmk,ckw->cmw', chosen, panel, preferred_element_type=jnp.floa...  10.8 us
  transfers between devices with their start and end apart: 4, of which 2 were waited for; matrix products, arithmetic and copies ran while one was open for 25% of the time, Pallas kernels for 0%

commit v1 on v0

--- a/solution.py
+++ b/solution.py
@@ -54,7 +54,9 @@
     packed = jnp.sum(lower_six * weight_six, axis=4).reshape(children, rows, local_pairs * TILE)
     flags = tile_mask.reshape(children, row_tiles, local_pairs, 2)[..., 1].astype(jnp.bfloat16)
     packed_full, flags_full = (
-        lax.all_gather(packed, "col", axis=2, tiled=True),
+        jnp.concatenate(
+            lax.all_to_all(jnp.stack([packed] * lax.axis_size("col")), "col", 0, 0), axis=2
+        ),
         lax.all_gather(flags, "col", axis=2, tiled=True),
     )
     total_pairs = flags_full.shape[2]

time: 344 us -> 363 us (1.055)
  waiting for transfers between devices: 166 us -> 146 us
  blocking collectives: 26.3 us -> 44 us
  starting transfers between devices: 18.9 us -> 27.5 us
  local copies, waits for them, and re-layouts: 64 us -> 72.6 us
  other arithmetic: 44.3 us -> 51.6 us
  matrix products: 10.8 us -> 6.68 us
    all_gather x1 -> x0, waiting for transfers between devices: 18.7 us -> none  [shards(): lax.all_gather(packed, 'col', axis=2, tiled=True)]
    all_gather x1, blocking collectives: 15.6 us -> 33.4 us  [shards(): lax.all_gather(flags, 'col', axis=2, tiled=True)]
    all_to_all x0 -> x1, starting transfers between devices: none -> 8.85 us  [shards(): lax.all_to_all(jnp.stack([packed] * lax.axis_size('col')), 'col', 0, 0)]
    mul x0 -> x1, other arithmetic: none -> 8.03 us  [shards(): packed_five * select[:, :, None, :, None]]
    all_to_all x0 -> x1, local copies, waits for them, and re-layouts: none -> 6.26 us  [shards(): lax.all_to_all(jnp.stack([packed] * lax.axis_size('col')), 'col', 0, 0)]
    dot_general x2, matrix products: 10.8 us -> 6.68 us  [shards(): jnp.einsum('cmk,ckw->cmw', chosen, panel, preferred_element_type=jnp.floa...]
  transfers between devices with their start and end apart: 4 -> 4, of which waited for: 2 -> 1; matrix products, arithmetic and copies ran while one was open for 25% -> 27% of each run, Pallas kernels for 0% -> 0%
where the time goes in v1:
time: 363 us; the launch traced here: 362 us
  waiting for transfers between devices  146 us (40%)
  local copies, waits for them, and re-layouts  72.6 us (20%)
  other arithmetic  51.6 us (14%)
  blocking collectives  44 us (12%)
  starting transfers between devices  27.5 us (8%)
  between operations  13.6 us (4%)
  matrix products  6.68 us (2%)
    all_to_all x1, waiting for transfers between devices, shards(): lax.all_to_all(values, ROW, split_axis=1, concat_axis=1, tiled=True)  145 us
    all_gather x1, blocking collectives, shards(): lax.all_gather(flags, 'col', axis=2, tiled=True)  33.4 us
    unnamed x24, local copies, waits for them, and re-layouts  25.8 us
    scatter-add x1, other arithmetic, assemble(): return result.at[index].add(values.reshape(-1, width), mode='drop')  22.1 us
    mul x4, local copies, waits for them, and re-layouts, shards(): packed_five * select[:, :, None, :, None]  19.7 us
    another operation x2, other arithmetic  18.1 us
    all_gather x1, blocking collectives, gathered_by_axis(): result = lax.all_gather(result, axes[number], axis=dim, tiled=True)  10.6 us
    all_to_all x1, starting transfers between devices, shards(): lax.all_to_all(places, ROW, split_axis=1, concat_axis=1, tiled=True)  9.38 us
  transfers between devices with their start and end apart: 4, of which 1 were waited for; matrix products, arithmetic and copies ran while one was open for 27% of the time, Pallas kernels for 0%

profile of v1, /device:TPU:103, one launch (start us, length us, event | category | flops | bytes accessed | tf_op | source)
XLA Modules:
  0.0 361.5 jit_solution(12113729253234978242)
XLA Ops:
  6.5 0.0 all-gather.3.cloned.1.call-start
  6.5 3.2 copy.77
  9.7 0.0 copy-done.4
  9.7 10.6 %all_gather.10 = bf16[2,256,512]{2,1,0:T(8,128)(2,1)} all-gather(bf16[2,64,512]{2,1,0:T(8,128)(2,1)S(1)} %copy-done.4), channel_id=1, replica_groups=mesh['row_0'=8,'row_1'=4,'col'=8] {'row_1'}, dimensions={1}, use_global_device_ids=true | all-gather | bytes 655360 | tf_op jit(solution)/shard_map/all_gather | solution.py:14
  20.3 0.0 all-gather.3.cloned.1.call-update
  20.4 0.0 copy-done.3
  20.4 0.3 reshape.102
  20.7 0.1 copy.48
  20.8 2.9 multiply_reduce_fusion
  23.8 2.8 stack.3
  26.5 8.9 %all-to-all-start.1 = ((bf16[8,2,1024,128]{3,2,1,0:T(8,128)(2,1)}), bf16[8,2,1024,128]{3,2,1,0:T(8,128)(2,1)}, u32[]{:S(2)}, u32[]{:S(2)}) async-start(bf16[8,2,1024,128]{3,2,1,0:T(8,128)(2,1)} %stack.3), calls=%async_computation.1 | async-start | bytes 8388608 | tf_op jit(solution)/shard_map/all_to_all | solution.py:58
  35.5 18.0 %reduce-window.6 = s32[2,32,8,128]{3,2,1,0:T(8,128)S(1)} reduce-window(s32[2,32,8,128]{3,2,1,0:T(8,128)S(1)} %fusion.3, s32[]{:T(128)} %constant.45.clone.1), window={size=1x1x1x128 pad=0_0x0_0x0_0x127_0}, to_apply=%region_0.0 | reduce-window | flops 8323072 | bytes 524292 | tf_op jit(solution)/shard_map/reduce-window
  53.5 0.1 slice.21
  53.6 0.2 copy.44
  53.8 0.1 copy.45
  53.9 0.1 add_add_fusion
  54.1 0.1 fusion.2
  54.2 0.1 multiply_reduce_fusion.1
  54.3 0.1 and_reduce_fusion
  54.5 33.4 %all-gather = bf16[2,8,8,1]{1,0,3,2:T(2,128)(2,1)S(1)} all-gather(bf16[2,8,1,1]{1,0,3,2:T(2,128)(2,1)S(1)} %copy.50), channel_id=2, replica_groups=mesh['row_0'=8,'row_1'=4,'col'=8] {'col'}, dimensions={2}, use_global_device_ids=true | all-gather | bytes 288 | tf_op jit(solution)/shard_map/all_gather | solution.py:60
  87.8 0.1 copy.51
  87.9 0.1 copy.52
  88.0 2.5 mul.52
  90.5 7.3 %mul.53 = bf16[2,1024,1024]{1,2,0:T(8,128)(2,1)} reshape(bf16[2,8,128,8,128]{2,1,4,3,0:T(8,128)(2,1)} %mul.52) | data formatting | bytes 8388608 | tf_op jit(solution)/shard_map/mul | solution.py:68
  97.9 0.1 copy.56
  97.9 2.6 mul.55
  100.5 7.3 %mul.56 = bf16[2,1024,1024]{1,2,0:T(8,128)(2,1)} reshape(bf16[2,8,128,8,128]{2,1,4,3,0:T(8,128)(2,1)} %mul.55) | data formatting | bytes 8388608 | tf_op jit(solution)/shard_map/mul | solution.py:68
  107.8 8.1 %scatter_custom_fusion.1 = f32[3072]{0:T(1024)S(1)} fusion(s32[2048]{0:T(1024)S(1)} %bitcast.69, f32[2048]{0:T(1024)S(1)} %bitcast.71, f32[]{:T(128)} %constant.43.clone.1), kind=kCustom, calls=%fused_computation.35 | custom fusion | bytes 12292
  115.9 0.1 reshape.101
  116.0 0.6 copy.46
  116.6 0.0 all-to-all-done.1
  116.6 9.4 %all-to-all-start = ((f32[2,32,48]{2,0,1:T(2,128)}), f32[2,32,48]{2,0,1:T(2,128)S(1)}, u32[]{:S(2)}, u32[]{:S(2)}) async-start(f32[2,32,48]{2,0,1:T(2,128)} %copy.46), calls=%async_computation | async-start | bytes 65536 | tf_op jit(solution)/shard_map/all_to_all | solution.py:81
  126.0 6.3 %copy.49 = bf16[8,2,1024,128]{2,3,0,1:T(8,128)(2,1)} copy(bf16[8,2,1024,128]{3,2,1,0:T(8,128)(2,1)} %all-to-all-done.1) | data formatting | bytes 8388608 | tf_op jit(solution)/shard_map/all_to_all | solution.py:58
  132.3 8.0 %bitcast_multiply_fusion = (bf16[2,1024,1024]{1,2,0:T(8,128)(2,1)}, bf16[2,1024,1024]{1,2,0:T(8,128)(2,1)}) fusion(bf16[2,1024,1024]{1,2,0:T(8,128)(2,1)} %mul.56, bf16[8,2,1024,128]{2,3,0,1:T(8,128)(2,1)} %copy.49, bf16[2,1024,1024]{1,2,0:T(8,128)(2,1)} %mul.53), kind=kLoop, calls=%fused_computation.3 | loop fusion | flops 4194304 | bytes 20971520 | tf_op jit(solution)/shard_map/mul | solution.py:68
  140.3 2.7 fusion.11
  143.0 0.8 copy-done.1
  143.7 2.4 fusion.12
  146.1 0.0 copy-done
  146.1 1.1 copy-done.2
  147.2 4.3 %add_subtract_fusion = f32[2,1024,512]{2,1,0:T(8,128)} fusion(f32[2,1024,512]{2,1,0:T(8,128)S(1)} %copy-done.2, f32[2,1024,512]{2,1,0:T(8,128)S(1)} %fusion.12, bf16[2,1024,1024]{1,2,0:T(8,128)(2,1)S(1)} %copy-done, bf16[2,1024,512]{2,1,0:T(8,128)(2,1)S(1)} %bitcast.60), kind=kOutput, calls=%fused_computation.5 | convolution fusion | flops 2149580800 | bytes 18874368 | tf_op jit(solution)/shard_map/cmk,ckw->cmw/dot_general | solution.py:72
  151.5 12.7 %scatter_custom_fusion.2 = f32[3072,512]{1,0:T(8,128)} fusion(s32[2048]{0:T(1024)S(1)} %bitcast.70, f32[2048,512]{1,0:T(8,128)} %bitcast.62, f32[]{:T(128)} %constant.52.clone.1), kind=kCustom, calls=%fused_computation.6 | custom fusion | bytes 6291968
  164.2 6.7 %copy.59 = f32[2,32,48,512]{3,2,0,1:T(8,128)} copy(f32[2,32,48,512]{3,2,1,0:T(8,128)} %bitcast.58) | data formatting | bytes 12582912 | tf_op jit(solution)/shard_map/reshape | solution.py:36
  170.9 0.0 all-to-all-done
  170.9 9.3 %all-to-all-start.2 = ((f32[2,32,48,512]{3,2,0,1:T(8,128)}), f32[2,32,48,512]{3,2,0,1:T(8,128)}, u32[]{:S(2)}, u32[]{:S(2)}) async-start(f32[2,32,48,512]{3,2,0,1:T(8,128)} %copy.59), calls=%async_computation.2 | async-start | bytes 12582912 | tf_op jit(solution)/shard_map/all_to_all | solution.py:80
  180.2 0.1 convert_element_type.48
  180.4 145.5 %all-to-all-done.2 = f32[2,32,48,512]{3,2,0,1:T(8,128)} async-done(((f32[2,32,48,512]{3,2,0,1:T(8,128)}), f32[2,32,48,512]{3,2,0,1:T(8,128)}, u32[]{:S(2)}, u32[]{:S(2)}) %all-to-all-start.2) | async-done | bytes 6291488 | tf_op jit(solution)/shard_map/all_to_all | solution.py:80
  325.8 6.8 %copy.60 = f32[2,32,48,512]{3,2,1,0:T(8,128)} copy(f32[2,32,48,512]{3,2,0,1:T(8,128)} %all-to-all-done.2) | data formatting | bytes 12582912 | tf_op jit(solution)/shard_map/all_to_all | solution.py:80
  332.6 22.1 %scatter_fusion = f32[1024,512]{1,0:T(8,128)} fusion(f32[1024,512]{1,0:T(8,128)} %copy.77, s32[3072]{0:T(1024)S(1)} %bitcast.66, f32[3072,512]{1,0:T(8,128)} %bitcast.59), kind=kCustom, calls=%fused_computation | custom fusion | flops 1572864 | bytes 18886656 | tf_op jit(solution)/shard_map/scatter-add | solution.py:42
  (32 shorter events, 0.3 us)
Async XLA Ops:
  6.5 3.2 copy-start.4
  6.5 13.8 %copy-start.3 = (bf16[2,1024,256]{2,1,0:T(8,128)(2,1)S(1)}, bf16[2,1024,256]{2,1,0:T(8,128)(2,1)}, u32[]{:S(2)}) copy-start(bf16[2,1024,256]{2,1,0:T(8,128)(2,1)} %param.7) | copy-start | bytes 3145732
  6.5 14.1 %copy-start.6 = (s32[2,8,2]{1,2,0:T(2,128)S(1)}, s32[2,8,2]{1,2,0:T(2,128)}, u32[]{:S(2)}) copy-start(s32[2,8,2]{1,2,0:T(2,128)} %param.9) | copy-start | bytes 388
  6.5 133.8 %all-gather.3.cloned.1.call-start = ((), (), s32[]{:S(2)}) async-start(), calls=%async_computation.3 | async-start | bytes 4718592 | tf_op jit(solution)/shard_map/all_gather | solution.py:14
  26.5 8.9 %copy-start.5 = (s32[2,1024]{1,0:T(2,128)S(1)}, s32[2,1024]{1,0:T(2,128)}, u32[]{:S(2)}) copy-start(s32[2,1024]{1,0:T(2,128)} %param.10) | copy-start | bytes 24580
  26.5 27.7 %copy-start.7 = (s32[2]{0:T(128)S(1)}, s32[2]{0:T(128)}, u32[]{:S(2)}) copy-start(s32[2]{0:T(128)} %constant.56) | copy-start | bytes 28
  26.5 27.8 %copy-start.8 = (s32[2]{0:T(128)S(1)}, s32[2]{0:T(128)}, u32[]{:S(2)}) copy-start(s32[2]{0:T(128)} %constant.59) | copy-start | bytes 28
  26.5 90.1 %all-to-all-start.1 = ((bf16[8,2,1024,128]{3,2,1,0:T(8,128)(2,1)}), bf16[8,2,1024,128]{3,2,1,0:T(8,128)(2,1)}, u32[]{:S(2)}, u32[]{:S(2)}) async-start(bf16[8,2,1024,128]{3,2,1,0:T(8,128)(2,1)} %stack.3), calls=%async_computation.1 | async-start | bytes 8388608 | tf_op jit(solution)/shard_map/all_to_all | solution.py:58
  116.6 54.3 %all-to-all-start = ((f32[2,32,48]{2,0,1:T(2,128)}), f32[2,32,48]{2,0,1:T(2,128)S(1)}, u32[]{:S(2)}, u32[]{:S(2)}) async-start(f32[2,32,48]{2,0,1:T(2,128)} %copy.46), calls=%async_computation | async-start | bytes 65536 | tf_op jit(solution)/shard_map/all_to_all | solution.py:81
  140.3 3.5 copy-start.1
  143.7 2.4 copy-start
  143.7 3.5 copy-start.2
  170.9 154.9 %all-to-all-start.2 = ((f32[2,32,48,512]{3,2,0,1:T(8,128)}), f32[2,32,48,512]{3,2,0,1:T(8,128)}, u32[]{:S(2)}, u32[]{:S(2)}) async-start(f32[2,32,48,512]{3,2,0,1:T(8,128)} %copy.59), calls=%async_computation.2 | async-start | bytes 12582912 | tf_op jit(solution)/shard_map/all_to_all | solution.py:80
Sparse Core Ops, SparseCore 0:
  20.5 59.1 all-gather.2
